TPU v7x, 128 devices: a whole 4x4x4 slice. The times are simulated.
128 devices in a mesh: section: 2 (over core), dp: 4 (over x), mp: 16 (over z, y).
Axes of the slice: x: 4, y: 4, z: 4, core: 2. Of those that a mesh axis runs over, the one named last changes fastest.
Arguments:
- segment_input: bfloat16 [2, 4, 256, 2048], P(None, 'dp', None, 'mp'), may hold values from -6 to 6
- out_grad: bfloat16 [2, 4, 256, 2048], P(None, 'dp', None, 'mp'), may hold values from -6 to 6
- pool_tokens: bfloat16 [16, 4, 128, 896], P('section', 'dp'), may hold values from -6 to 6
- neighbour_ids: int32 [2, 4, 4, 4], P(None, 'dp'), may hold values from 0 to 15, as said below
- neighbour_counts: int32 [2, 4, 4], P(None, 'dp'), may hold values from 1 to 4
- enc_gain: float32 [896], replicated, may hold values from 0.5 to 1.5
- enc_up: bfloat16 [896, 4096], P(None, 'mp'), may hold values from -0.1875 to 0.1875
- enc_down: bfloat16 [4096, 896], P(None, 'mp'), may hold values from -0.09375 to 0.09375
- norm_gain: float32 [2, 2048], P('section'), may hold values from 0.5 to 1.5
- w_query: bfloat16 [2, 2048, 4096], P('section', None, 'mp'), may hold values from -0.125 to 0.125
- w_key: bfloat16 [2, 896, 4096], P('section', None, 'mp'), may hold values from -0.1875 to 0.1875
- w_value: bfloat16 [2, 896, 4096], P('section', None, 'mp'), may hold values from -0.1875 to 0.1875
- w_out: bfloat16 [2, 4096, 2048], P('section', None, 'mp'), may hold values from -0.09375 to 0.09375
Outputs:
- grad_key: bfloat16 [2, 896, 4096], P('section', None, 'mp')
- grad_value: bfloat16 [2, 896, 4096], P('section', None, 'mp')
Inputs may be any that keep to these rules, and one draw needn't show every extreme that they name: `neighbour_ids`: the 4 slots of one stretch name distinct pool stretches.
All inputs are finite; a program needn't handle non-finite values.
Results may differ from a plain program's by a relative error of at most 0.025.
Values may be sent and summed in bfloat16 or wider, within the bound.
A program may use at most 128 MiB of HBM per device.

v0:
```python
import jax
import jax.numpy as jnp
from jax import lax
from jax.sharding import PartitionSpec as P

HEAD = 128
NT = 128


EPSILON = 1e-05


def passed_along(value, axis, by):
    peers = lax.axis_size(axis)
    pairs = [(i, i + by) for i in range(peers) if 0 <= i + by < peers]
    return lax.ppermute(value, axis, pairs)


def rms_scale(values):
    return lax.rsqrt(jnp.mean(values * values, axis=-1, keepdims=True) + EPSILON)


def collect(tensor):
    return lax.all_gather(tensor, "mp", axis=1, tiled=True)


def collect_pair(first, second):
    return (
        lax.all_gather(first, "mp", axis=1, tiled=True),
        lax.all_gather(second, "mp", axis=1, tiled=True),
    )


def pass_on(tensor, offset):
    return passed_along(tensor, "section", offset)


def attend(queries, key_block, value_block, usable):
    scores = jnp.einsum("cqhe,ckhe->chqk", queries, key_block, preferred_element_type=jnp.float32)
    scores = jnp.where(usable[:, None, None, :], scores, -1e30)
    weights = jax.nn.softmax(scores, axis=-1)
    weights_bf = weights.astype(jnp.bfloat16)
    attended = jnp.einsum(
        "chqk,ckhe->cqhe", weights_bf, value_block, preferred_element_type=jnp.float32
    )
    return (weights, weights_bf, attended.astype(jnp.bfloat16))


def attend_back(queries, key_block, value_block, weights, weights_bf, grad_attended):
    grad_weights = jnp.einsum(
        "cqhe,ckhe->chqk", grad_attended, value_block, preferred_element_type=jnp.float32
    )
    grad_scores = weights * (grad_weights - jnp.sum(weights * grad_weights, axis=-1, keepdims=True))
    grad_values = jnp.einsum(
        "chqk,cqhe->ckhe", weights_bf, grad_attended, preferred_element_type=jnp.float32
    ).astype(jnp.bfloat16)
    grad_keys = jnp.einsum("chqk,cqhe->ckhe", grad_scores, queries.astype(jnp.float32)).astype(
        jnp.bfloat16
    )
    grad_queries = jnp.einsum("chqk,ckhe->cqhe", grad_scores, key_block.astype(jnp.float32))
    return (grad_keys, grad_values, grad_queries)


def front(rows_in, gain_full, query_cols, key_block, value_block, usable, head_count):
    rows_wide = rows_in.astype(jnp.float32)
    inv_rms = rms_scale(rows_wide)
    normed = (rows_wide * inv_rms * gain_full).astype(jnp.bfloat16)
    query_raw = jnp.dot(normed, query_cols, preferred_element_type=jnp.float32)
    queries = (query_raw * HEAD ** (-0.5)).astype(jnp.bfloat16)
    queries = queries.reshape(key_block.shape[0], -1, head_count, HEAD)
    weights, weights_bf, attended = attend(queries, key_block, value_block, usable)
    return (inv_rms, query_raw, queries, weights, weights_bf, attended)


def on_device(
    segment_input,
    out_grad,
    pool_tokens,
    neighbour_ids,
    neighbour_counts,
    enc_gain,
    enc_up,
    enc_down,
    norm_gain,
    w_query,
    w_key,
    w_value,
    w_out,
):
    model_count = lax.axis_size("mp")
    model_index = lax.axis_index("mp")
    segment_count = lax.axis_size("section")
    segment_index = lax.axis_index("section")
    micro_count = segment_input.shape[0]
    row_count = segment_input.shape[2]
    feat_count = segment_input.shape[3]
    width = feat_count * model_count
    head_count = w_query.shape[2] // HEAD
    tract_count = neighbour_ids.shape[2]
    key_span = neighbour_ids.shape[3] * NT
    raw_rows = pool_tokens[:, 0].reshape(-1, pool_tokens.shape[3])
    raw_wide = raw_rows.astype(jnp.float32)
    enc_normed = (raw_wide * rms_scale(raw_wide) * enc_gain).astype(jnp.bfloat16)
    hidden_part = jax.nn.gelu(
        jnp.dot(enc_normed, enc_up, preferred_element_type=jnp.float32)
    ).astype(jnp.bfloat16)
    hidden_full = collect(hidden_part)
    enc_feat = enc_down.shape[1]
    raw_slice = lax.dynamic_slice_in_dim(raw_wide, model_index * enc_feat, enc_feat, 1)
    encoded = (
        raw_slice + jnp.dot(hidden_full, enc_down, preferred_element_type=jnp.float32)
    ).astype(jnp.bfloat16)
    slot_ids = neighbour_ids[:, 0].reshape(-1)
    shard_rows = encoded.shape[0]
    token_index = jnp.arange(NT, dtype=jnp.int32)
    global_rows = ((slot_ids * NT)[:, None] + token_index[None, :]).reshape(-1)
    empty_pool = jnp.zeros((segment_count * shard_rows, enc_feat * model_count), jnp.bfloat16)
    portion = lax.all_gather(encoded, ("section", "mp"), axis=0, tiled=True)
    shard_total = portion.shape[0] // shard_rows

    def one_shard(position, whole_pool):
        shard_block = lax.dynamic_slice_in_dim(portion, position * shard_rows, shard_rows, 0)
        row_start = position // model_count * shard_rows
        col_start = position % model_count * enc_feat
        return lax.dynamic_update_slice(whole_pool, shard_block, (row_start, col_start))

    whole_pool = lax.fori_loop(0, shard_total, one_shard, empty_pool)
    neighbours = jnp.take(whole_pool, global_rows, axis=0)

    def project(weight):
        projected = jnp.dot(neighbours, weight[0], preferred_element_type=jnp.float32).astype(
            jnp.bfloat16
        )
        return projected.reshape(micro_count, tract_count, key_span, head_count, HEAD)

    key_all = project(w_key)
    value_all = project(w_value)
    span_index = jnp.arange(key_span, dtype=jnp.int32) // NT
    usable_all = span_index[None, None, :] < neighbour_counts[:, 0][:, :, None]
    query_cols = w_query[0]
    out_cols = w_out[0]
    query_rows, out_rows = (
        lax.all_to_all(query_cols, "mp", split_axis=0, concat_axis=1, tiled=True),
        lax.all_to_all(out_cols, "mp", split_axis=0, concat_axis=1, tiled=True),
    )
    gain_full = norm_gain[0]
    gain_own = lax.dynamic_slice_in_dim(gain_full, model_index * feat_count, feat_count, 0)
    inputs_own = segment_input[:, 0]
    grads_own = out_grad[:, 0]
    step_count = micro_count + segment_count - 1
    empty_share = jnp.zeros((row_count, feat_count), jnp.bfloat16)
    stored_start = jnp.zeros((micro_count, row_count, width), jnp.bfloat16)

    def forward_step(step, state):
        received, stored = state
        which = step - segment_index
        active = (which >= 0) & (which < micro_count)
        which = jnp.clip(which, 0, micro_count - 1)
        incoming = jnp.where(segment_index == 0, inputs_own[which], received)
        rows_full = collect(incoming)
        outputs = front(
            rows_full,
            gain_full,
            query_cols,
            key_all[which],
            value_all[which],
            usable_all[which],
            head_count,
        )
        attended = collect(outputs[5].reshape(row_count, -1))
        result = incoming.astype(jnp.float32) + jnp.dot(
            attended, out_cols, preferred_element_type=jnp.float32
        )
        stored = stored.at[which].set(jnp.where(active, rows_full, stored[which]))
        return (pass_on(result.astype(jnp.bfloat16), 1), stored)

    _, stored = lax.fori_loop(0, step_count, forward_step, (empty_share, stored_start))
    grad_start = jnp.zeros((micro_count, tract_count, key_span, head_count, HEAD), jnp.bfloat16)

    def backward_step(step, state):
        received, key_grads, value_grads = state
        which = step - (segment_count - 1 - segment_index)
        active = (which >= 0) & (which < micro_count)
        which = jnp.clip(which, 0, micro_count - 1)
        incoming = jnp.where(segment_index == segment_count - 1, grads_own[which], received)
        rows_full = stored[which]
        rows_own = lax.dynamic_slice_in_dim(rows_full, model_index * feat_count, feat_count, 1)
        key_block = key_all[which]
        value_block = value_all[which]
        inv_rms, query_raw, queries, weights, weights_bf, _ = front(
            rows_full, gain_full, query_cols, key_block, value_block, usable_all[which], head_count
        )
        grad_full = collect(incoming)
        grad_att = jnp.dot(grad_full, out_rows.T, preferred_element_type=jnp.float32).astype(
            jnp.bfloat16
        )
        grad_att = grad_att.reshape(queries.shape)
        grad_keys, grad_values, grad_queries = attend_back(
            queries, key_block, value_block, weights, weights_bf, grad_att
        )
        grad_scaled = (grad_queries * HEAD ** (-0.5)).reshape(row_count, -1).astype(jnp.bfloat16)
        part_total = jnp.sum(
            grad_scaled.astype(jnp.float32) * query_raw, axis=1, keepdims=True
        ).astype(jnp.bfloat16)
        scaled_full, totals = collect_pair(grad_scaled, part_total)
        row_total = jnp.sum(totals.astype(jnp.float32), axis=1, keepdims=True)
        grad_normed = jnp.dot(scaled_full, query_rows.T, preferred_element_type=jnp.float32)
        rows_wide = rows_own.astype(jnp.float32)
        grad_in = (
            incoming.astype(jnp.float32)
            + inv_rms * gain_own * grad_normed
            - rows_wide * inv_rms * inv_rms * row_total / width
        )
        key_grads = key_grads.at[which].set(jnp.where(active, grad_keys, key_grads[which]))
        value_grads = value_grads.at[which].set(jnp.where(active, grad_values, value_grads[which]))
        return (pass_on(grad_in.astype(jnp.bfloat16), -1), key_grads, value_grads)

    _, key_grads, value_grads = lax.fori_loop(
        0, step_count, backward_step, (empty_share, grad_start, grad_start)
    )
    contract = (((0,), (0,)), ((), ()))
    key_sum = lax.dot_general(
        neighbours,
        key_grads.reshape(-1, head_count * HEAD),
        contract,
        preferred_element_type=jnp.float32,
    )
    value_sum = lax.dot_general(
        neighbours,
        value_grads.reshape(-1, head_count * HEAD),
        contract,
        preferred_element_type=jnp.float32,
    )
    key_total, value_total = (
        lax.psum(key_sum.astype(jnp.bfloat16), "dp").astype(jnp.float32),
        lax.psum(value_sum.astype(jnp.bfloat16), "dp").astype(jnp.float32),
    )
    return (key_total.astype(jnp.bfloat16)[None], value_total.astype(jnp.bfloat16)[None])


def solution(mesh):
    placed = (
        P(None, "dp", None, "mp"),
        P(None, "dp", None, "mp"),
        P("section", "dp", None, None),
        P(None, "dp", None, None),
        P(None, "dp", None),
        P(),
        P(None, "mp"),
        P(None, "mp"),
        P("section", None),
        P("section", None, "mp"),
        P("section", None, "mp"),
        P("section", None, "mp"),
        P("section", None, "mp"),
    )
    return jax.shard_map(
        on_device,
        mesh=mesh,
        in_specs=placed,
        out_specs=(P("section", None, "mp"), P("section", None, "mp")),
        check_vma=False,
    )
```

profile of v0, /device:TPU:0, one launch (start us, length us, event | category | flops | bytes accessed | tf_op | source)
XLA Modules:
  0.0 1101.6 jit_solution(5113289207940649873)
XLA Ops:
  16.3 80.0 %all-gather.10.cloned.1.call-done = bf16[1024,4096]{1,0:T(8,128)(2,1)} async-done(((bf16[1024,256]{1,0:T(8,128)(2,1)}), bf16[1024,4096]{1,0:T(8,128)(2,1)}) %all-gather.10.cloned.1.call-update) | async-done | bytes 8388624 | tf_op jit(solution)/shard_map/all_gather | solution.py:24
  96.3 6.7 fusion.104
  103.0 5.1 all-to-all-start
  108.5 17.1 %all-to-all-done = bf16[16,256,128]{2,1,0:T(8,128)(2,1)S(1)} async-done(((bf16[16,256,128]{2,1,0:T(8,128)(2,1)}), bf16[16,256,128]{2,1,0:T(8,128)(2,1)S(1)}, u32[]{:S(2)}, u32[]{:S(2)}) %all-to-all-start) | async-done | bytes 1048608 | tf_op jit(solution)/shard_map/all_to_all | solution.py:144
  133.1 13.0 %all-to-all-done.1 = bf16[16,128,256]{2,1,0:T(8,128)(2,1)S(1)} async-done(((bf16[16,128,256]{2,1,0:T(8,128)(2,1)}), bf16[16,128,256]{2,1,0:T(8,128)(2,1)S(1)}, u32[]{:S(2)}, u32[]{:S(2)}) %all-to-all-start.1) | async-done | bytes 1048608 | tf_op jit(solution)/shard_map/all_to_all | solution.py:143
  148.1 6.3 all-gather.12.cloned.1.call-done
  156.6 184.6 %while.54 = (s32[]{:T(128)}, bf16[2048,896]{1,0:T(8,128)(2,1)}, bf16[32768,56]{0,1:T(8,128)(2,1)}, s32[]{:T(128)}, s32[]{:T(128)}, /*index=5*/s32[]{:T(128)}, s3...) while((s32[]{:T(128)}, bf16[2048,896]{1,0:T(8,128)(2,1)}, ...), condition=%wide.region_2.3_spmd, body=%wide.region_1.2_spmd.sunk | while | flops 26 | bytes 688530 | solution.py:127
  157.7 4.6 dynamic_update_slice.11
  163.4 5.2 dynamic_update_slice.11
  169.7 5.2 dynamic_update_slice.11
  176.0 5.2 dynamic_update_slice.11
  182.3 5.2 dynamic_update_slice.11
  188.6 5.3 dynamic_update_slice.11
  195.0 5.3 dynamic_update_slice.11
  201.3 5.2 dynamic_update_slice.11
  207.7 5.2 dynamic_update_slice.11
  214.0 5.2 dynamic_update_slice.11
  220.3 5.2 dynamic_update_slice.11
  226.6 5.2 dynamic_update_slice.11
  232.9 5.2 dynamic_update_slice.11
  239.2 5.2 dynamic_update_slice.11
  245.5 4.6 dynamic_update_slice.11
  251.2 4.6 dynamic_update_slice.11
  261.6 4.3 dynamic_update_slice.11
  267.1 4.3 dynamic_update_slice.11
  272.5 4.3 dynamic_update_slice.11
  277.9 4.3 dynamic_update_slice.11
  283.3 4.3 dynamic_update_slice.11
  341.2 22.4 %gather_fusion = bf16[4096,896]{1,0:T(8,128)(2,1)} fusion(bf16[2048,896]{1,0:T(8,128)(2,1)} %get-tuple-element.835, s32[4096]{0:T(1024)S(1)} %broadcast_clamp_fusion), kind=kCustom, calls=%fused_computation | custom fusion | bytes 14696448 | tf_op jit(solution)/shard_map/jit(_take)/gather | solution.py:128
  363.6 5.8 convolution_convert_fusion.4
  373.8 5.7 convolution_convert_fusion.5
  385.3 318.6 %while.55 = (s32[]{:T(128)}, bf16[256,128]{1,0:T(8,128)(2,1)S(1)}, bf16[2,256,2048]{2,1,0:T(8,128)(2,1)}, pred[]{:T(512)}, s32[]{:T(128)}, /*index=5*/bf16[2,256...) while((s32[]{:T(128)}, bf16[256,128]{1,0:T(8,128)(2,1)S(1)}, ...), condition=%wide.region_8.9_spmd, body=%wide.region_3.8_spmd.sunk | while | flops 677446400 | bytes 32006564 | solution.py:177
  386.1 45.0 %all-gather.14.cloned.1.call-done = bf16[256,2048]{1,0:T(8,128)(2,1)} async-done(((bf16[256,128]{1,0:T(8,128)(2,1)}), bf16[256,2048]{1,0:T(8,128)(2,1)}) %all-gather.14.cloned.1.call-update) | async-done | bytes 1048592 | tf_op jit(solution)/shard_map/while/body/eval_jaxpr/all_gather | solution.py:24
  441.1 44.5 %all-gather.16.cloned.1.call-done = bf16[256,4096]{1,0:T(8,128)(2,1)} async-done(((bf16[256,256]{1,0:T(8,128)(2,1)}), bf16[256,4096]{1,0:T(8,128)(2,1)}) %all-gather.16.cloned.1.call-update) | async-done | bytes 2097168 | tf_op jit(solution)/shard_map/while/body/eval_jaxpr/all_gather | solution.py:24
  492.2 45.0 %all-gather.14.cloned.1.call-done = bf16[256,2048]{1,0:T(8,128)(2,1)} async-done(((bf16[256,128]{1,0:T(8,128)(2,1)}), bf16[256,2048]{1,0:T(8,128)(2,1)}) %all-gather.14.cloned.1.call-update) | async-done | bytes 1048592 | tf_op jit(solution)/shard_map/while/body/eval_jaxpr/all_gather | solution.py:24
  547.2 44.5 %all-gather.16.cloned.1.call-done = bf16[256,4096]{1,0:T(8,128)(2,1)} async-done(((bf16[256,256]{1,0:T(8,128)(2,1)}), bf16[256,4096]{1,0:T(8,128)(2,1)}) %all-gather.16.cloned.1.call-update) | async-done | bytes 2097168 | tf_op jit(solution)/shard_map/while/body/eval_jaxpr/all_gather | solution.py:24
  598.3 45.2 %all-gather.14.cloned.1.call-done = bf16[256,2048]{1,0:T(8,128)(2,1)} async-done(((bf16[256,128]{1,0:T(8,128)(2,1)}), bf16[256,2048]{1,0:T(8,128)(2,1)}) %all-gather.14.cloned.1.call-update) | async-done | bytes 1048592 | tf_op jit(solution)/shard_map/while/body/eval_jaxpr/all_gather | solution.py:24
  653.6 44.5 %all-gather.16.cloned.1.call-done = bf16[256,4096]{1,0:T(8,128)(2,1)} async-done(((bf16[256,256]{1,0:T(8,128)(2,1)}), bf16[256,4096]{1,0:T(8,128)(2,1)}) %all-gather.16.cloned.1.call-update) | async-done | bytes 2097168 | tf_op jit(solution)/shard_map/while/body/eval_jaxpr/all_gather | solution.py:24
  708.8 323.1 %while.56 = (s32[]{:T(128)}, bf16[256,128]{1,0:T(8,128)(2,1)S(1)}, bf16[2,4,512,2,128]{4,3,2,1,0:T(2,128)(2,1)}, bf16[2,4,512,2,128]{4,3,2,1,0:T(2,128)(2,1)}, p...) while((s32[]{:T(128)}, bf16[256,128]{1,0:T(8,128)(2,1)S(1)}, ...), condition=%wide.region_17.18_spmd, body=%wide.region_9.17_spmd.sunk | while | flops 1152261888 | bytes 76540544 | solution.py:218
  715.5 39.3 %all-gather.18.cloned.1.call-done = bf16[256,2048]{1,0:T(8,128)(2,1)} async-done(((bf16[256,128]{1,0:T(8,128)(2,1)}), bf16[256,2048]{1,0:T(8,128)(2,1)}) %all-gather.18.cloned.1.call-update) | async-done | bytes 1048592 | tf_op jit(solution)/shard_map/while/body/eval_jaxpr/all_gather | solution.py:24
  782.7 22.8 %all-gather.2 = bf16[16,1,256]{2,1,0:T(2,128)(2,1)S(1)} all-gather(bf16[1,1,256]{2,1,0:T(2,128)(2,1)S(1)} %reshape.462), channel_id=1, replica_groups=mesh['section'=2,'dp'=4,'mp'=16] {'mp'}, dimensions={0}, use_global_device_ids=true | all-gather | bytes 8704 | tf_op jit(solution)/shard_map/while/body/eval_jaxpr/all_gather | solution.py:30
  822.7 40.1 %all-gather.18.cloned.1.call-done = bf16[256,2048]{1,0:T(8,128)(2,1)} async-done(((bf16[256,128]{1,0:T(8,128)(2,1)}), bf16[256,2048]{1,0:T(8,128)(2,1)}) %all-gather.18.cloned.1.call-update) | async-done | bytes 1048592 | tf_op jit(solution)/shard_map/while/body/eval_jaxpr/all_gather | solution.py:24
  890.7 22.8 %all-gather.2 = bf16[16,1,256]{2,1,0:T(2,128)(2,1)S(1)} all-gather(bf16[1,1,256]{2,1,0:T(2,128)(2,1)S(1)} %reshape.462), channel_id=1, replica_groups=mesh['section'=2,'dp'=4,'mp'=16] {'mp'}, dimensions={0}, use_global_device_ids=true | all-gather | bytes 8704 | tf_op jit(solution)/shard_map/while/body/eval_jaxpr/all_gather | solution.py:30
  930.7 40.1 %all-gather.18.cloned.1.call-done = bf16[256,2048]{1,0:T(8,128)(2,1)} async-done(((bf16[256,128]{1,0:T(8,128)(2,1)}), bf16[256,2048]{1,0:T(8,128)(2,1)}) %all-gather.18.cloned.1.call-update) | async-done | bytes 1048592 | tf_op jit(solution)/shard_map/while/body/eval_jaxpr/all_gather | solution.py:24
  998.7 22.8 %all-gather.2 = bf16[16,1,256]{2,1,0:T(2,128)(2,1)S(1)} all-gather(bf16[1,1,256]{2,1,0:T(2,128)(2,1)S(1)} %reshape.462), channel_id=1, replica_groups=mesh['section'=2,'dp'=4,'mp'=16] {'mp'}, dimensions={0}, use_global_device_ids=true | all-gather | bytes 8704 | tf_op jit(solution)/shard_map/while/body/eval_jaxpr/all_gather | solution.py:30
  1031.9 7.4 fusion.101
  1039.3 6.7 fusion.98
  1046.1 45.3 %all-reduce.3.cloned.1.call-done = (bf16[1,896,256]{2,1,0:T(8,128)(2,1)}, bf16[1,896,256]{2,1,0:T(8,128)(2,1)}) async-done(((bf16[1,896,256]{2,1,0:T(8,128)(2,1)}, bf16[1,896,256]{2,1,0:T(8,128)(2,1)}), (bf16[1,896,256]{2,1,0:T(8,128)(2,1)}, bf16[1,896,256]{2,1,0:T(8,128)(2,1)})) %all-reduce.3.cloned.1.call-update) | async-done | bytes 917520 | tf_op jit(solution)/shard_map/psum | solution.py:235
  (354 shorter events, 304.4 us)
Async XLA Ops:
  7.2 356.4 %copy-start = (bf16[1,896,256]{2,1,0:T(8,128)(2,1)S(1)}, bf16[1,896,256]{2,1,0:T(8,128)(2,1)}, u32[]{:S(2)}) copy-start(bf16[1,896,256]{2,1,0:T(8,128)(2,1)} %param.35) | copy-start | bytes 1376260
  7.2 89.1 %all-gather.10.cloned.1.call-start = ((), (), s32[]{:S(2)}) async-start(), calls=%async_computation.2 | async-start | bytes 8912896 | tf_op jit(solution)/shard_map/all_gather | solution.py:24
  9.3 2.9 copy-start.16
  12.3 84.0 %copy-start.12 = (bf16[4096,56]{0,1:T(8,128)(2,1)S(1)}, bf16[4096,56]{0,1:T(8,128)(2,1)}, u32[]{:S(2)}) copy-start(bf16[4096,56]{0,1:T(8,128)(2,1)} %param.32) | copy-start | bytes 1376260
  16.3 138.2 %all-gather.12.cloned.1.call-start = ((), (), s32[]{:S(2)}) async-start(), calls=%async_computation.3 | async-start | bytes 3784704 | tf_op jit(solution)/shard_map/all_gather | solution.py:118
  103.0 5.1 copy-start.14
  103.0 5.2 copy-start.18
  103.0 5.3 copy-start.15
  103.0 22.6 %all-to-all-start = ((bf16[16,256,128]{2,1,0:T(8,128)(2,1)}), bf16[16,256,128]{2,1,0:T(8,128)(2,1)S(1)}, u32[]{:S(2)}, u32[]{:S(2)}) async-start(bf16[16,256,128]{2,1,0:T(8,128)(2,1)} %bitcast.38), calls=%async_computation | async-start | bytes 2097152 | tf_op jit(solution)/shard_map/all_to_all | solution.py:144
  125.6 20.5 %all-to-all-start.1 = ((bf16[16,128,256]{2,1,0:T(8,128)(2,1)}), bf16[16,128,256]{2,1,0:T(8,128)(2,1)S(1)}, u32[]{:S(2)}, u32[]{:S(2)}) async-start(bf16[16,128,256]{2,1,0:T(8,128)(2,1)} %bitcast.41), calls=%async_computation.1 | async-start | bytes 2097152 | tf_op jit(solution)/shard_map/all_to_all | solution.py:143
  385.3 45.8 %all-gather.14.cloned.1.call-start = ((), (), s32[]{:S(2)}) async-start(), calls=%async_computation.5 | async-start | bytes 1114112 | tf_op jit(solution)/shard_map/while/body/eval_jaxpr/all_gather | solution.py:24
  386.0 99.5 %all-gather.16.cloned.1.call-start = ((), (), s32[]{:S(2)}) async-start(), calls=%async_computation.6 | async-start | bytes 2228224 | tf_op jit(solution)/shard_map/while/body/eval_jaxpr/all_gather | solution.py:24
  438.2 47.4 %copy-start.8 = (bf16[256,128]{1,0:T(8,128)(2,1)S(1)}, bf16[256,128]{1,0:T(8,128)(2,1)}, u32[]{:S(2)}) copy-start(bf16[256,128]{1,0:T(8,128)(2,1)} %bitcast_select_fusion.6) | copy-start | bytes 196612 | tf_op jit(solution)/shard_map/while
  441.1 48.3 %copy-start.2 = (bf16[256,2048]{1,0:T(8,128)(2,1)S(1)}, bf16[256,2048]{1,0:T(8,128)(2,1)}, u32[]{:S(2)}) copy-start(bf16[256,2048]{1,0:T(8,128)(2,1)} %all-gather.14.cloned.1.call-done) | copy-start | bytes 3145732 | tf_op jit(solution)/shard_map/while
  488.2 3.3 collective-permute-start
  491.5 45.7 %all-gather.14.cloned.1.call-start = ((), (), s32[]{:S(2)}) async-start(), calls=%async_computation.5 | async-start | bytes 1114112 | tf_op jit(solution)/shard_map/while/body/eval_jaxpr/all_gather | solution.py:24
  492.1 99.6 %all-gather.16.cloned.1.call-start = ((), (), s32[]{:S(2)}) async-start(), calls=%async_computation.6 | async-start | bytes 2228224 | tf_op jit(solution)/shard_map/while/body/eval_jaxpr/all_gather | solution.py:24
  544.3 47.4 %copy-start.8 = (bf16[256,128]{1,0:T(8,128)(2,1)S(1)}, bf16[256,128]{1,0:T(8,128)(2,1)}, u32[]{:S(2)}) copy-start(bf16[256,128]{1,0:T(8,128)(2,1)} %bitcast_select_fusion.6) | copy-start | bytes 196612 | tf_op jit(solution)/shard_map/while
  547.2 48.3 %copy-start.2 = (bf16[256,2048]{1,0:T(8,128)(2,1)S(1)}, bf16[256,2048]{1,0:T(8,128)(2,1)}, u32[]{:S(2)}) copy-start(bf16[256,2048]{1,0:T(8,128)(2,1)} %all-gather.14.cloned.1.call-done) | copy-start | bytes 3145732 | tf_op jit(solution)/shard_map/while
  594.2 3.3 collective-permute-start
  597.5 46.0 %all-gather.14.cloned.1.call-start = ((), (), s32[]{:S(2)}) async-start(), calls=%async_computation.5 | async-start | bytes 1114112 | tf_op jit(solution)/shard_map/while/body/eval_jaxpr/all_gather | solution.py:24
  598.3 99.8 %all-gather.16.cloned.1.call-start = ((), (), s32[]{:S(2)}) async-start(), calls=%async_computation.6 | async-start | bytes 2228224 | tf_op jit(solution)/shard_map/while/body/eval_jaxpr/all_gather | solution.py:24
  650.7 47.4 %copy-start.8 = (bf16[256,128]{1,0:T(8,128)(2,1)S(1)}, bf16[256,128]{1,0:T(8,128)(2,1)}, u32[]{:S(2)}) copy-start(bf16[256,128]{1,0:T(8,128)(2,1)} %bitcast_select_fusion.6) | copy-start | bytes 196612 | tf_op jit(solution)/shard_map/while
  653.6 48.3 %copy-start.2 = (bf16[256,2048]{1,0:T(8,128)(2,1)S(1)}, bf16[256,2048]{1,0:T(8,128)(2,1)}, u32[]{:S(2)}) copy-start(bf16[256,2048]{1,0:T(8,128)(2,1)} %all-gather.14.cloned.1.call-done) | copy-start | bytes 3145732 | tf_op jit(solution)/shard_map/while
  700.6 3.3 collective-permute-start
  703.9 4.8 copy-start.11
  704.0 4.8 copy-start.20
  708.8 46.0 %all-gather.18.cloned.1.call-start = ((), (), s32[]{:S(2)}) async-start(), calls=%async_computation.7 | async-start | bytes 1114112 | tf_op jit(solution)/shard_map/while/body/eval_jaxpr/all_gather | solution.py:24
  709.5 98.6 %all-gather.20.cloned.1.call-start = ((), (), s32[]{:S(2)}) async-start(), calls=%async_computation.8 | async-start | bytes 2228224 | tf_op jit(solution)/shard_map/while/body/eval_jaxpr/all_gather | solution.py:29
  765.5 4.8 copy-start.3
  780.2 27.9 %copy-start.7 = (bf16[256,128]{1,0:T(8,128)(2,1)S(1)}, bf16[256,128]{1,0:T(8,128)(2,1)}, u32[]{:S(2)}) copy-start(bf16[256,128]{1,0:T(8,128)(2,1)} %bitcast_select_fusion.7) | copy-start | bytes 196612 | tf_op jit(solution)/shard_map/while
  808.1 4.0 copy-start.4
  810.8 3.8 collective-permute-start.1
  815.9 46.8 %all-gather.18.cloned.1.call-start = ((), (), s32[]{:S(2)}) async-start(), calls=%async_computation.7 | async-start | bytes 1114112 | tf_op jit(solution)/shard_map/while/body/eval_jaxpr/all_gather | solution.py:24
  816.7 99.4 %all-gather.20.cloned.1.call-start = ((), (), s32[]{:S(2)}) async-start(), calls=%async_computation.8 | async-start | bytes 2228224 | tf_op jit(solution)/shard_map/while/body/eval_jaxpr/all_gather | solution.py:29
  873.5 4.8 copy-start.3
  888.1 27.9 %copy-start.7 = (bf16[256,128]{1,0:T(8,128)(2,1)S(1)}, bf16[256,128]{1,0:T(8,128)(2,1)}, u32[]{:S(2)}) copy-start(bf16[256,128]{1,0:T(8,128)(2,1)} %bitcast_select_fusion.7) | copy-start | bytes 196612 | tf_op jit(solution)/shard_map/while
  916.1 4.0 copy-start.4
  918.8 3.8 collective-permute-start.1
  923.9 46.8 %all-gather.18.cloned.1.call-start = ((), (), s32[]{:S(2)}) async-start(), calls=%async_computation.7 | async-start | bytes 1114112 | tf_op jit(solution)/shard_map/while/body/eval_jaxpr/all_gather | solution.py:24
  924.6 99.4 %all-gather.20.cloned.1.call-start = ((), (), s32[]{:S(2)}) async-start(), calls=%async_computation.8 | async-start | bytes 2228224 | tf_op jit(solution)/shard_map/while/body/eval_jaxpr/all_gather | solution.py:29
  981.5 4.8 copy-start.3
  996.1 27.9 %copy-start.7 = (bf16[256,128]{1,0:T(8,128)(2,1)S(1)}, bf16[256,128]{1,0:T(8,128)(2,1)}, u32[]{:S(2)}) copy-start(bf16[256,128]{1,0:T(8,128)(2,1)} %bitcast_select_fusion.7) | copy-start | bytes 196612 | tf_op jit(solution)/shard_map/while
  1024.0 4.0 copy-start.4
  1026.8 3.8 collective-permute-start.1
  1031.9 59.5 %all-reduce.3.cloned.1.call-start = ((), (), s32[]{:S(2)}) async-start(), calls=%async_computation.4 | async-start | bytes 1835008 | tf_op jit(solution)/shard_map/psum | solution.py:235
  1031.9 7.4 copy-start.6
  1039.3 55.7 %copy-start.1 = (bf16[1,896,256]{2,1,0:T(8,128)(2,1)S(1)}, bf16[1,896,256]{2,1,0:T(8,128)(2,1)}, u32[]{:S(2)}) copy-start(bf16[1,896,256]{2,1,0:T(8,128)(2,1)} %param.35) | copy-start | bytes 1376260
  (11 other events, 20.1 us)
Sparse Core Ops, SparseCore 0:
  16.4 79.8 all-gather.9
  103.2 51.2 all-gather.11
  388.8 42.2 all-gather.13
  439.2 46.3 all-gather.15
  494.6 42.4 all-gather.13
  545.2 46.3 all-gather.15
  601.0 42.5 all-gather.13
  651.6 46.3 all-gather.15
  712.3 42.5 all-gather.17
  761.7 46.3 all-gather.19
  819.4 43.2 all-gather.17
  869.6 46.3 all-gather.19
  927.4 43.3 all-gather.17
  977.6 46.3 all-gather.19
  1046.2 45.1 all-reduce.2
where the time goes:
time: 1110 us; the launch traced here: 1100 us
  waiting for transfers between devices  558 us (50%)
  local copies, waits for them, and re-layouts  296 us (27%)
  matrix products  120 us (11%)
  blocking collectives  68.5 us (6%)
  other arithmetic  26 us (2%)
  starting transfers between devices  17 us (2%)
  between operations  13.9 us (1%)
    all_gather x10, waiting for transfers between devices, collect(): return lax.all_gather(tensor, 'mp', axis=1, tiled=True)  468 us
    dynamic_update_slice x32, local copies, waits for them, and re-layouts, one_shard(): lax.dynamic_update_slice(whole_pool, shard_block, (row_start, col_start))  149 us
    all_gather x3, blocking collectives, collect_pair(): lax.all_gather(second, 'mp', axis=1, tiled=True)  68.5 us
    psum x1, waiting for transfers between devices, on_device(): lax.psum(key_sum.astype(jnp.bfloat16), 'dp').astype(jnp.float32)  45.3 us
    dynamic_slice x64, local copies, waits for them, and re-layouts, one_shard(): lax.dynamic_slice_in_dim(portion, position * shard_rows, shard_rows, 0)  34.4 us
    gather x1, local copies, waits for them, and re-layouts, on_device(): neighbours = jnp.take(whole_pool, global_rows, axis=0)  22.4 us
  transfers between devices with their start and end apart: 23, of which 17 were waited for; matrix products, arithmetic and copies ran while one was open for 10% of the time, Pallas kernels for 0%

commit v1 on v0

v1 whole, which is shorter than its diff:
```python
import functools

import jax
import jax.numpy as jnp
from jax import lax
from jax.experimental import pallas as pl
from jax.experimental.pallas import tpu as pltpu
from jax.sharding import PartitionSpec as P

HEAD = 128
NT = 128
SIDE = 4
EPSILON = 1e-05
SCALE = HEAD ** (-0.5)
VMEM = pltpu.VMEM
BF = jnp.bfloat16
F32 = jnp.float32
LIMIT = 60 * 1024 * 1024

OFFSETS = [(2, 2), (2, 1), (2, 3), (1, 2), (3, 2), (1, 1), (3, 3), (1, 3), (3, 1),
           (2, 0), (0, 2), (1, 0), (0, 1), (3, 0), (0, 3)]


def dims(lhs, rhs):
    return (((lhs,), (rhs,)), ((), ()))


def mul(a, b, lhs=1, rhs=0):
    return lax.dot_general(a, b, dims(lhs, rhs), preferred_element_type=F32)


def rms_scale(values):
    return lax.rsqrt(jnp.mean(values * values, axis=-1, keepdims=True) + EPSILON)


def shifted(m, dz, dy):
    z = lax.rem(lax.div(m, SIDE) + dz, SIDE)
    y = lax.rem(lax.rem(m, SIDE) + dy, SIDE)
    return z * SIDE + y


def to_peer(m, k):
    return shifted(m, *OFFSETS[k])


def from_peer(m, k):
    dz, dy = OFFSETS[k]
    return shifted(m, (SIDE - dz) % SIDE, (SIDE - dy) % SIDE)


def remote(src, dst, send, recv, device):
    return pltpu.make_async_remote_copy(
        src_ref=src, dst_ref=dst, send_sem=send, recv_sem=recv,
        device_id=device, device_id_type=pl.DeviceIdType.MESH,
    )


def greet(devices):
    barrier = pltpu.get_barrier_semaphore()
    for device in devices:
        pl.semaphore_signal(
            barrier, inc=1, device_id=device, device_id_type=pl.DeviceIdType.MESH
        )
    pl.semaphore_wait(barrier, len(devices))


def rows_of(index, size):
    return pl.ds(pl.multiple_of(index * size, size), size)


def encode_kernel(
    x_ref, wo_ref, ed_ref, pool_ref, gain_ref, up_ref,
    enc_ref, xf_ref, wor_ref,
    edr, dt, hid, part, rs,
    own_sem, ed_s, ed_r, x_s, x_r, wo_s, wo_r, rs_s, rs_r, ag_s, ag_r, fw_s, fw_r,
):
    s = lax.axis_index("section")
    m = lax.axis_index("mp")
    other = {"section": 1 - s}
    count = len(OFFSETS)
    greet([{"mp": to_peer(m, k)} for k in range(count)] + [other])
    span = wor_ref.shape[0]
    cols = rows_of(m, HEAD)
    own = [
        pltpu.make_async_copy(x_ref, xf_ref.at[:, cols], own_sem.at[0]),
        pltpu.make_async_copy(wo_ref.at[rows_of(m, span), :], wor_ref.at[:, cols], own_sem.at[1]),
        pltpu.make_async_copy(ed_ref.at[m], edr.at[m], own_sem.at[2]),
    ]
    for copy in own:
        copy.start()
    sends = []
    for k in range(count):
        p = to_peer(m, k)
        sends.append(remote(ed_ref.at[p], edr.at[m], ed_s.at[k], ed_r.at[k], {"mp": p}))
        sends[-1].start()
    for k in range(count):
        p = to_peer(m, k)
        sends.append(remote(wo_ref.at[rows_of(p, span), :], wor_ref.at[:, cols],
                            wo_s.at[k], wo_r.at[k], {"mp": p}))
        sends[-1].start()
        sends.append(remote(x_ref, xf_ref.at[:, cols], x_s.at[k], x_r.at[k], {"mp": p}))
        sends[-1].start()

    gain = gain_ref[...]

    def hidden_rows(i, carry):
        rows = rows_of(i, 256)
        wide = pool_ref[rows, :].astype(F32)
        normed = (wide * rms_scale(wide) * gain).astype(BF)
        hid[rows, :] = jax.nn.gelu(mul(normed, up_ref[...])).astype(BF)
        return carry

    lax.fori_loop(0, SIDE, hidden_rows, 0)

    own[2].wait()
    for k in range(count):
        p = from_peer(m, k)
        remote(ed_ref.at[p], edr.at[p], ed_s.at[k], ed_r.at[k], {"mp": p}).wait_recv()
    feat = enc_ref.shape[1] // len(edr)
    for p in range(len(edr)):
        dt[pl.ds(p * feat, feat), :] = edr[p, pl.ds(0, feat), :].astype(F32)
    down = dt[...].astype(BF)
    shard = rs.shape[1]
    for dz in (2, 1, 3, 0):
        block = rows_of(lax.rem(lax.div(m, SIDE) + dz, SIDE), SIDE * shard)
        part[block, :] = mul(hid[block, :], down, 1, 1).astype(BF)
        for k in range(count):
            if OFFSETS[k][0] != dz:
                continue
            p = to_peer(m, k)
            sends.append(remote(part.at[rows_of(p, shard), :], rs.at[k],
                                rs_s.at[k], rs_r.at[k], {"mp": p}))
            sends[-1].start()
    mine = rows_of(m, shard)
    total = pool_ref[mine, :].astype(F32) + part[mine, :].astype(F32)
    for k in range(count):
        p = from_peer(m, k)
        remote(part.at[rows_of(p, shard), :], rs.at[k], rs_s.at[k], rs_r.at[k], {"mp": p}).wait_recv()
        total = total + rs[k].astype(F32)
    half = s * len(edr)
    place = rows_of(half + m, shard)
    enc_ref[place, :] = total.astype(BF)
    for k in range(count):
        p = to_peer(m, k)
        sends.append(remote(enc_ref.at[place, :], enc_ref.at[place, :],
                            ag_s.at[k], ag_r.at[k], {"mp": p}))
        sends[-1].start()
    sends.append(remote(enc_ref.at[place, :], enc_ref.at[place, :],
                        fw_s.at[count], fw_r.at[count], other))
    sends[-1].start()
    for k in reversed(range(count)):
        p = from_peer(m, k)
        there = rows_of(half + p, shard)
        remote(enc_ref.at[there, :], enc_ref.at[there, :], ag_s.at[k], ag_r.at[k], {"mp": p}).wait_recv()
        sends.append(remote(enc_ref.at[there, :], enc_ref.at[there, :],
                            fw_s.at[k], fw_r.at[k], other))
        sends[-1].start()
    away = (1 - s) * len(edr)
    for k in range(count + 1):
        p = m if k == count else from_peer(m, k)
        there = rows_of(away + p, shard)
        remote(enc_ref.at[there, :], enc_ref.at[there, :], fw_s.at[k], fw_r.at[k], other).wait_recv()
    for k in range(count):
        p = from_peer(m, k)
        there = rows_of(p, HEAD)
        remote(wo_ref.at[rows_of(p, span), :], wor_ref.at[:, there],
               wo_s.at[k], wo_r.at[k], {"mp": p}).wait_recv()
        remote(x_ref, xf_ref.at[:, there], x_s.at[k], x_r.at[k], {"mp": p}).wait_recv()
    own[0].wait()
    own[1].wait()
    for copy in sends:
        copy.wait_send()


def encode(x, wo, ed, pool, gain, up):
    peers, _, span = ed.shape
    rows, enc = pool.shape
    dma = pltpu.SemaphoreType.DMA
    count = len(OFFSETS)
    vmem = pl.BlockSpec(memory_space=VMEM)
    hbm = pl.BlockSpec(memory_space=pl.ANY)
    return pl.pallas_call(
        encode_kernel,
        name="encode_exchange",
        out_shape=(
            jax.ShapeDtypeStruct((2 * rows, enc), BF),
            jax.ShapeDtypeStruct((x.shape[0], x.shape[1] * peers), BF),
            jax.ShapeDtypeStruct((span, wo.shape[1] * peers), BF),
        ),
        in_specs=[hbm, hbm, hbm, vmem, vmem, vmem],
        out_specs=(vmem,) * 3,
        scratch_shapes=[
            VMEM(ed.shape, BF), VMEM((enc, span), F32), VMEM((rows, span), BF),
            VMEM((rows, enc), BF), VMEM((count, rows // peers, enc), BF),
            dma((3,)),
        ] + [dma((count,))] * 10 + [dma((count + 1,))] * 2,
        compiler_params=pltpu.CompilerParams(
            collective_id=0, has_side_effects=True, vmem_limit_bytes=LIMIT),
    )(x, wo, ed, pool, gain, up)


def head_cols(h):
    return pl.ds(h * HEAD, HEAD)


def gathered(ref, ids_ref, c, columns):
    slots = ids_ref.shape[1]
    return jnp.concatenate(
        [ref[rows_of(ids_ref[c, j], NT), columns] for j in range(slots)], axis=0)


def soft(scores, used):
    slot = lax.div(lax.broadcasted_iota(jnp.int32, scores.shape, 1), NT)
    scores = jnp.where(slot < used, scores, -1e30)
    grown = jnp.exp(scores - jnp.max(scores, axis=-1, keepdims=True))
    return grown / jnp.sum(grown, axis=-1, keepdims=True)


def queries_of(x_ref, gain_ref, wq_ref, q_ref):
    def some(i, carry):
        rows = rows_of(i, 256)
        wide = x_ref[rows, :].astype(F32)
        normed = (wide * rms_scale(wide) * gain_ref[...]).astype(BF)
        q_ref[rows, :] = (mul(normed, wq_ref[...]) * SCALE).astype(BF)
        return carry

    lax.fori_loop(0, x_ref.shape[0] // 256, some, 0)


def grad_attended(x_ref, wor_ref, ga_ref):
    def some(i, carry):
        rows = rows_of(i, 256)
        ga_ref[rows, :] = mul(x_ref[rows, :], wor_ref[...], 1, 1).astype(BF)
        return carry

    lax.fori_loop(0, x_ref.shape[0] // 256, some, 0)


def front_kernel(ids_ref, used_ref, x_ref, gain_ref, wq_ref, enc_ref, wk_ref, wv_ref, wor_ref,
                 k_ref, v_ref, q_ref, p_ref, part_ref, ga_ref):
    s = lax.axis_index("section")

    def project(i, carry):
        rows = rows_of(i, 512)
        block = enc_ref[rows, :]
        k_ref[rows, :] = mul(block, wk_ref[...]).astype(BF)
        v_ref[rows, :] = mul(block, wv_ref[...]).astype(BF)
        return carry

    lax.fori_loop(0, enc_ref.shape[0] // 512, project, 0)
    heads = q_ref.shape[1] // HEAD
    tracts = ids_ref.shape[0]
    size = x_ref.shape[0] // tracts

    @pl.when(s == 0)
    def _():
        queries_of(x_ref, gain_ref, wq_ref, q_ref)

        def tract(c, carry):
            rows = rows_of(c, size)
            found = []
            for h in range(heads):
                keys = gathered(k_ref, ids_ref, c, head_cols(h))
                probs = soft(mul(q_ref[rows, head_cols(h)], keys, 1, 1), used_ref[c])
                p_ref[c, h] = probs
                values = gathered(v_ref, ids_ref, c, head_cols(h))
                found.append(mul(probs.astype(BF), values).astype(BF))
            part_ref[rows, :] = mul(jnp.concatenate(found, axis=1), wor_ref[...]).astype(BF)
            return carry

        lax.fori_loop(0, tracts, tract, 0)

    @pl.when(s != 0)
    def _():
        grad_attended(x_ref, wor_ref, ga_ref)


def back_tract(c, rows, heads, ids_ref, enc_ref, k_ref, v_ref, q_ref, ga_ref, probs_of, acc_k, acc_v,
               scores_used):
    near = gathered(enc_ref, ids_ref, c, slice(None))
    key_t, value_t, query_g = [], [], []
    for h in range(heads):
        q = q_ref[rows, head_cols(h)]
        ga = ga_ref[rows, head_cols(h)]
        values = gathered(v_ref, ids_ref, c, head_cols(h))
        keys = None
        if k_ref is not None:
            keys = gathered(k_ref, ids_ref, c, head_cols(h))
        probs = probs_of(h, q, keys)
        grad_probs = mul(ga, values, 1, 1)
        grad_scores = probs * (grad_probs - jnp.sum(probs * grad_probs, axis=-1, keepdims=True))
        grad_scores = grad_scores.astype(BF)
        value_t.append(mul(ga, probs.astype(BF), 0, 0).astype(BF))
        key_t.append(mul(q, grad_scores, 0, 0).astype(BF))
        if keys is not None:
            query_g.append((mul(grad_scores, keys) * SCALE).astype(BF))
    acc_k[...] += mul(jnp.concatenate(key_t, axis=0), near)
    acc_v[...] += mul(jnp.concatenate(value_t, axis=0), near)
    return query_g


def late_kernel(ids_ref, used_ref, x_ref, gain_ref, wq_ref, enc_ref, k_ref, v_ref, ga_ref,
                part_ref, sk_ref, sv_ref, q_ref, acc_k, acc_v):
    heads = q_ref.shape[1] // HEAD
    tracts = ids_ref.shape[0]
    size = x_ref.shape[0] // tracts

    @pl.when(lax.axis_index("section") != 0)
    def _():
        queries_of(x_ref, gain_ref, wq_ref, q_ref)
        acc_k[...] = jnp.zeros_like(acc_k)
        acc_v[...] = jnp.zeros_like(acc_v)

        def tract(c, carry):
            rows = rows_of(c, size)

            def probs_of(h, q, keys):
                return soft(mul(q, keys, 1, 1), used_ref[c])

            query_g = back_tract(c, rows, heads, ids_ref, enc_ref, k_ref, v_ref, q_ref, ga_ref,
                                 probs_of, acc_k, acc_v, None)
            part_ref[rows, :] = mul(jnp.concatenate(query_g, axis=1), wq_ref[...], 1, 1).astype(BF)
            return carry

        lax.fori_loop(0, tracts, tract, 0)
        sk_ref[...] = jnp.transpose(acc_k[...]).astype(BF)
        sv_ref[...] = jnp.transpose(acc_v[...]).astype(BF)


def early_kernel(ids_ref, g_ref, wor_ref, enc_ref, v_ref, q_ref, p_ref, lk_ref, lv_ref,
                 sk_ref, sv_ref, ga_ref, acc_k, acc_v):
    heads = q_ref.shape[1] // HEAD
    tracts = ids_ref.shape[0]
    size = g_ref.shape[0] // tracts
    s = lax.axis_index("section")

    @pl.when(s == 0)
    def _():
        grad_attended(g_ref, wor_ref, ga_ref)
        acc_k[...] = jnp.zeros_like(acc_k)
        acc_v[...] = jnp.zeros_like(acc_v)

        def tract(c, carry):
            rows = rows_of(c, size)

            def probs_of(h, q, keys):
                return p_ref[c, h]

            back_tract(c, rows, heads, ids_ref, enc_ref, None, v_ref, q_ref, ga_ref,
                       probs_of, acc_k, acc_v, None)
            return carry

        lax.fori_loop(0, tracts, tract, 0)
        sk_ref[...] = jnp.transpose(acc_k[...]).astype(BF)
        sv_ref[...] = jnp.transpose(acc_v[...]).astype(BF)

    @pl.when(s != 0)
    def _():
        sk_ref[...] = lk_ref[...]
        sv_ref[...] = lv_ref[...]


def relay_kernel(from_section, combine, *refs):
    part_ref, row_refs, full_ref = refs[0], refs[1:-8], refs[-8]
    rs, done, rs_s, rs_r, ag_s, ag_r = refs[-7:-1]
    s = lax.axis_index("section")
    m = lax.axis_index("mp")
    count = len(OFFSETS)
    there = {"section": 1 - s}
    everyone = [{"mp": to_peer(m, k)} for k in range(count)]
    everyone += [{"mp": to_peer(m, k), "section": 1 - s} for k in range(count)]
    greet(everyone + [there])
    shard = rs.shape[1]
    mine = rows_of(m, shard)

    @pl.when(s == from_section)
    def _():
        sends = []
        for k in range(count):
            p = to_peer(m, k)
            sends.append(remote(part_ref.at[rows_of(p, shard), :], rs.at[k],
                                rs_s.at[k], rs_r.at[k], {"mp": p}))
            sends[-1].start()
        total = part_ref[mine, :].astype(F32)
        for k in range(count):
            p = from_peer(m, k)
            remote(part_ref.at[rows_of(p, shard), :], rs.at[k],
                   rs_s.at[k], rs_r.at[k], {"mp": p}).wait_recv()
            total = total + rs[k].astype(F32)
        done[...] = combine(total, mine, *row_refs).astype(BF)
        for k in range(count + 1):
            device = there if k == count else {"mp": to_peer(m, k), "section": 1 - s}
            sends.append(remote(done, full_ref.at[mine, :], ag_s.at[k], ag_r.at[k], device))
            sends[-1].start()
        for copy in sends:
            copy.wait_send()

    @pl.when(s != from_section)
    def _():
        for k in range(count + 1):
            p = m if k == count else from_peer(m, k)
            device = there if k == count else {"mp": p, "section": 1 - s}
            remote(done, full_ref.at[rows_of(p, shard), :],
                   ag_s.at[k], ag_r.at[k], device).wait_recv()


def relay(from_section, combine, part, rows, ident, peers):
    dma = pltpu.SemaphoreType.DMA
    count = len(OFFSETS)
    vmem = pl.BlockSpec(memory_space=VMEM)
    shard = part.shape[0] // peers
    return pl.pallas_call(
        functools.partial(relay_kernel, from_section, combine),
        name="relay_%d" % ident,
        out_shape=jax.ShapeDtypeStruct(part.shape, BF),
        in_specs=[vmem] * (1 + len(rows)),
        out_specs=vmem,
        scratch_shapes=[
            VMEM((count, shard, part.shape[1]), BF), VMEM((shard, part.shape[1]), BF),
            dma((count,)), dma((count,)), dma((count + 1,)), dma((count + 1,)),
            VMEM((8, 128), F32),
        ],
        compiler_params=pltpu.CompilerParams(
            collective_id=ident, has_side_effects=True, vmem_limit_bytes=LIMIT),
    )(part, *rows)


def forward_rows(total, mine, x_ref):
    return x_ref[mine, :].astype(F32) + total


def backward_rows(total, mine, a_ref, g_ref, gain_ref):
    wide = a_ref[mine, :].astype(F32)
    inv = rms_scale(wide)
    gain = gain_ref[...]
    normed = (wide * inv * gain).astype(BF).astype(F32)
    row_total = jnp.sum(normed * total, axis=-1, keepdims=True)
    return (g_ref[mine, :].astype(F32) + inv * gain * total
            - wide * (inv * inv * row_total / wide.shape[1]))


def settle_kernel(k_ref, v_ref, ok_ref, ov_ref, rs, rs_s, rs_r, ag_s, ag_r):
    d = lax.axis_index("dp")
    count = SIDE - 1
    steps = (2, 1, 3)
    greet([{"dp": lax.rem(d + step, SIDE)} for step in steps])
    quarter = rs.shape[2]
    sends = []
    for k in range(count):
        p = lax.rem(d + steps[k], SIDE)
        for i, ref in enumerate((k_ref, v_ref)):
            sends.append(remote(ref.at[rows_of(p, quarter), :], rs.at[k, i],
                                rs_s.at[k, i], rs_r.at[k, i], {"dp": p}))
            sends[-1].start()
    mine = rows_of(d, quarter)
    for i, (ref, out) in enumerate(((k_ref, ok_ref), (v_ref, ov_ref))):
        total = ref[mine, :].astype(F32)
        for k in range(count):
            p = lax.rem(d + SIDE - steps[k], SIDE)
            remote(ref.at[mine, :], rs.at[k, i], rs_s.at[k, i], rs_r.at[k, i], {"dp": p}).wait_recv()
            total = total + rs[k, i].astype(F32)
        out[mine, :] = total.astype(BF)
        for k in range(count):
            p = lax.rem(d + steps[k], SIDE)
            sends.append(remote(out.at[mine, :], out.at[mine, :],
                                ag_s.at[k, i], ag_r.at[k, i], {"dp": p}))
            sends[-1].start()
    for i, out in enumerate((ok_ref, ov_ref)):
        for k in range(count):
            p = lax.rem(d + SIDE - steps[k], SIDE)
            there = rows_of(p, quarter)
            remote(out.at[there, :], out.at[there, :], ag_s.at[k, i], ag_r.at[k, i], {"dp": p}).wait_recv()
    for copy in sends:
        copy.wait_send()


def settle(keys, values):
    dma = pltpu.SemaphoreType.DMA
    vmem = pl.BlockSpec(memory_space=VMEM)
    count = SIDE - 1
    return pl.pallas_call(
        settle_kernel,
        name="settle",
        out_shape=(jax.ShapeDtypeStruct(keys.shape, BF),) * 2,
        in_specs=[vmem] * 2,
        out_specs=(vmem,) * 2,
        scratch_shapes=[VMEM((count, 2, keys.shape[0] // SIDE, keys.shape[1]), BF)]
        + [dma((count, 2))] * 4,
        compiler_params=pltpu.CompilerParams(
            collective_id=3, has_side_effects=True, vmem_limit_bytes=LIMIT),
    )(keys, values)


def local(kernel, name, outs, args, scalars, scratch=()):
    vmem = pl.BlockSpec(memory_space=VMEM)
    smem = pl.BlockSpec(memory_space=pltpu.SMEM)
    return pl.pallas_call(
        kernel,
        name=name,
        out_shape=tuple(jax.ShapeDtypeStruct(*o) for o in outs),
        in_specs=[smem] * scalars + [vmem] * (len(args) - scalars),
        out_specs=(vmem,) * len(outs),
        scratch_shapes=list(scratch),
        compiler_params=pltpu.CompilerParams(vmem_limit_bytes=LIMIT),
    )(*args)


def on_device(
    segment_input,
    out_grad,
    pool_tokens,
    neighbour_ids,
    neighbour_counts,
    enc_gain,
    enc_up,
    enc_down,
    norm_gain,
    w_query,
    w_key,
    w_value,
    w_out,
):
    peers = lax.axis_size("mp")
    s = lax.axis_index("section")
    micro, _, row_count, feat = segment_input.shape
    rows = micro * row_count
    width = feat * peers
    enc = pool_tokens.shape[3]
    head_width = w_query.shape[2]
    heads = head_width // HEAD
    tracts = micro * neighbour_ids.shape[2]
    slots = neighbour_ids.shape[3]
    size = rows // tracts
    ids = neighbour_ids[:, 0].reshape(tracts, slots)
    used = neighbour_counts[:, 0].reshape(tracts)
    x_own = jnp.where(s == 0, segment_input[:, 0], out_grad[:, 0]).reshape(rows, feat)
    pool = pool_tokens[:, 0].reshape(-1, enc)
    down = jnp.transpose(enc_down.reshape(peers, head_width, -1), (0, 2, 1))
    down = jnp.pad(down, ((0, 0), (0, -down.shape[1] % 16), (0, 0)))
    wq, wk, wv = w_query[0], w_key[0], w_value[0]

    encoded, x_full, wo_rows = encode(x_own, w_out[0], down, pool, enc_gain[None], enc_up)
    shape_q = ((rows, head_width), BF)
    shape_kv = ((encoded.shape[0], head_width), BF)
    keys, values, queries, probs, part, grad_att = local(
        front_kernel, "front",
        [shape_kv, shape_kv, shape_q, ((tracts, heads, size, slots * NT), F32),
         ((rows, width), BF), shape_q],
        (ids, used, x_full, norm_gain, wq, encoded, wk, wv, wo_rows), 2)
    acts = relay(0, forward_rows, part, (x_full,), 1, peers)
    shape_w = ((enc, head_width), BF)
    accs = [VMEM((head_width, enc), F32)] * 2
    part_back, late_k, late_v = local(
        late_kernel, "late",
        [((rows, width), BF), shape_w, shape_w],
        (ids, used, acts, norm_gain, wq, encoded, keys, values, grad_att), 2,
        [VMEM(*shape_q)] + accs)
    grads = relay(1, backward_rows, part_back, (acts, x_full, norm_gain), 2, peers)
    sum_k, sum_v = local(
        early_kernel, "early",
        [shape_w, shape_w],
        (ids, grads, wo_rows, encoded, values, queries, probs, late_k, late_v), 1,
        [VMEM(*shape_q)] + accs)
    grad_k, grad_v = settle(sum_k, sum_v)
    return (grad_k[None], grad_v[None])


def solution(mesh):
    placed = (
        P(None, "dp", None, "mp"),
        P(None, "dp", None, "mp"),
        P("section", "dp", None, None),
        P(None, "dp", None, None),
        P(None, "dp", None),
        P(),
        P(None, "mp"),
        P(None, "mp"),
        P("section", None),
        P("section", None, "mp"),
        P("section", None, "mp"),
        P("section", None, "mp"),
        P("section", None, "mp"),
    )
    return jax.shard_map(
        on_device,
        mesh=mesh,
        in_specs=placed,
        out_specs=(P("section", None, "mp"), P("section", None, "mp")),
        check_vma=False,
    )
```

time: 1110 us -> 276 us (0.25)
  waiting for transfers between devices: 558 us -> 0 us
  local copies, waits for them, and re-layouts: 296 us -> 7.99 us
  Pallas kernels: 0 us -> 264 us
  matrix products: 120 us -> 0 us
  blocking collectives: 68.5 us -> 0 us
  other arithmetic: 26 us -> 2.92 us
  starting transfers between devices: 17 us -> 0 us
  between operations: 13.9 us -> 0.68 us
    all_gather x14 -> x0, waiting for transfers between devices: 482 us -> none  [the longest x10 468 us: collect(): return lax.all_gather(tensor, 'mp', axis=1, tiled=True)]
    pallas_call x0 -> x7, Pallas kernels: none -> 264 us  [the longest x1 107 us: encode(): pl.pallas_call(encode_kernel, name='encode_exchange', out_shape=(jax.Shap...]
    dynamic_update_slice x32 -> x0, local copies, waits for them, and re-layouts: 149 us -> none  [one_shard(): lax.dynamic_update_slice(whole_pool, shard_block, (row_start, col_start))]
    dot_general x36 -> x0, matrix products: 109 us -> none  [the longest x6 12.7 us: front(): query_raw = jnp.dot(normed, query_cols, preferred_element_type=jnp.float32)]
    all_gather x3 -> x0, blocking collectives: 68.5 us -> none  [collect_pair(): lax.all_gather(second, 'mp', axis=1, tiled=True)]
    dynamic_slice x80 -> x0, local copies, waits for them, and re-layouts: 62.2 us -> none  [the longest x64 34.4 us: one_shard(): lax.dynamic_slice_in_dim(portion, position * shard_rows, shard_rows, 0)]
    psum x1 -> x0, waiting for transfers between devices: 45.3 us -> none  [on_device(): lax.psum(key_sum.astype(jnp.bfloat16), 'dp').astype(jnp.float32)]
    all_to_all x2 -> x0, waiting for transfers between devices: 30.2 us -> none  [the longest x1 17.1 us: on_device(): lax.all_to_all(out_cols, 'mp', split_axis=0, concat_axis=1, tiled=True)]
  transfers between devices with their start and end apart: 23 -> 0, of which waited for: 17 -> 0; matrix products, arithmetic and copies ran while one was open for 10% -> 0% of each run, Pallas kernels for 0% -> 0%
where the time goes in v1:
time: 276 us
  Pallas kernels  264 us (96%)
  local copies, waits for them, and re-layouts  7.99 us (3%)
  other arithmetic  2.92 us (1%)
    pallas_call x1, Pallas kernels, encode(): pl.pallas_call(encode_kernel, name='encode_exchange', out_shape=(jax.Shap...  107 us
    pallas_call x2, Pallas kernels, relay(): pl.pallas_call(functools.partial(relay_kernel, from_section, combine), na...  96.9 us
    pallas_call x3, Pallas kernels, local(): pl.pallas_call(kernel, name=name, out_shape=tuple((jax.ShapeDtypeStruct(*...  41.2 us
    pallas_call x1, Pallas kernels, settle(): pl.pallas_call(settle_kernel, name='settle', out_shape=(jax.ShapeDtypeStr...  19.7 us

profile of v1, /device:TPU:0, one launch (start us, length us, event | category | flops | bytes accessed | tf_op | source)
XLA Modules:
  0.0 276.1 jit_solution(3431619640340825273)
XLA Ops:
  0.6 0.5 broadcast.8
  1.1 1.3 reduce.3
  2.5 0.7 reshape_squeeze.10.used_ref
  3.2 1.3 broadcast_in_dim.9.gain_ref
  4.4 1.6 broadcast_select_fusion
  6.0 1.0 copy.27
  7.1 0.9 pad.4.ed_ref
  7.9 106.7 %encode_exchange.1 = (bf16[2048,896]{1,0:T(8,128)(2,1)}, bf16[512,2048]{1,0:T(8,128)(2,1)}, bf16[256,2048]{1,0:T(8,128)(2,1)}) custom-call(bf16[512,128]{1,0:T(8,128)(2,1)} %bitcast.21, bf16[4096,128]{1,0:T(8,128)(2,1)} %bitcast.20, bf16[16,64,256]{2,1,0:T(8,128)(2,1)} %pad.4.ed_ref, bf16[1024,896]{1,0:T(8,128)(2,1)} %bitcast.19, ...), custom_call_target="tpu_custom_call" | custom-call | tf_op jit(solution)/shard_map/encode_exchange/pallas_call | solution.py:182
  114.6 19.0 %front.1 = (bf16[2048,256]{1,0:T(8,128)(2,1)}, bf16[2048,256]{1,0:T(8,128)(2,1)}, bf16[512,256]{1,0:T(8,128)(2,1)}, f32[8,2,64,512]{3,2,1,0:T(8,128)}, bf16[512,...) custom-call(s32[8,4]{1,0:T(8,128)} %bitcast.27, s32[8]{0:T(128)} %reshape_squeeze.10.used_ref, ...), custom_call_target="tpu_custom_call" | custom-call | tf_op jit(solution)/shard_map/front/pallas_call | solution.py:497
  133.6 38.6 %relay_1.1.x_ref.refs_1_ = bf16[512,2048]{1,0:T(8,128)(2,1)} custom-call(bf16[512,2048]{1,0:T(8,128)(2,1)} %get-tuple-element.21.refs_0_, bf16[512,2048]{1,0:T(8,128)(2,1)} %get-tuple-element.18.x_ref.refs_1_.refs_2_), custom_call_target="tpu_custom_call" | custom-call | tf_op jit(solution)/shard_map/relay_1/pallas_call | solution.py:412
  172.3 5.2 %late.1 = (bf16[512,2048]{1,0:T(8,128)(2,1)}, bf16[896,256]{1,0:T(8,128)(2,1)}, bf16[896,256]{1,0:T(8,128)(2,1)}) custom-call(s32[8,4]{1,0:T(8,128)} %bitcast.28, s32[8]{0:T(128)} %reshape_squeeze.10.used_ref, bf16[512,2048]{1,0:T(8,128)(2,1)} %relay_1.1.x_ref.refs_1_, f32[1,2048]{1,0:T(1,128)} %refs_3_.1, bf16[2048,256]{1,0:T(8,128)(2,1)} %bitcast.17, ...), custom_call_target="tpu_custom_call" | custom-call | tf_op jit(solution)/shard_map/late/pallas_call | solution.py:497
  177.5 58.3 %relay_2.1.g_ref = bf16[512,2048]{1,0:T(8,128)(2,1)} custom-call(bf16[512,2048]{1,0:T(8,128)(2,1)} %get-tuple-element.25.refs_0_, bf16[512,2048]{1,0:T(8,128)(2,1)} %relay_1.1.x_ref.refs_1_, bf16[512,2048]{1,0:T(8,128)(2,1)} %get-tuple-element.18.x_ref.refs_1_.refs_2_, f32[1,2048]{1,0:T(1,128)} %refs_3_.1), custom_call_target="tpu_custom_call" | custom-call | tf_op jit(solution)/shard_map/relay_2/pallas_call | solution.py:412
  235.8 16.9 %early.1 = (bf16[896,256]{1,0:T(8,128)(2,1)}, bf16[896,256]{1,0:T(8,128)(2,1)}) custom-call(s32[8,4]{1,0:T(8,128)} %bitcast.29, bf16[512,2048]{1,0:T(8,128)(2,1)} %relay_2.1.g_ref, bf16[256,2048]{1,0:T(8,128)(2,1)} %get-tuple-element.20.wor_ref, bf16[2048,896]{1,0:T(8,128)(2,1)} %get-tuple-element.19.enc_ref, bf16[2048,256]{1,0:T(8,128)(2,1)} %get-tuple-element.23.v_ref, ...), custom_call_target="tpu_custom_call" | custom-call | tf_op jit(solution)/shard_map/early/pallas_call | solution.py:497
  252.7 19.7 %settle.1 = (bf16[896,256]{1,0:T(8,128)(2,1)}, bf16[896,256]{1,0:T(8,128)(2,1)}) custom-call(bf16[896,256]{1,0:T(8,128)(2,1)} %get-tuple-element.30.k_ref, bf16[896,256]{1,0:T(8,128)(2,1)} %get-tuple-element.31.v_ref), custom_call_target="tpu_custom_call" | custom-call | tf_op jit(solution)/shard_map/settle/pallas_call | solution.py:481
  272.4 1.8 copy.30
  274.2 1.8 copy.31

commit v2 on v1

--- a/solution.py
+++ b/solution.py
@@ -68,11 +68,172 @@
     return pl.ds(pl.multiple_of(index * size, size), size)
 
 
+def near(m, axis, step):
+    return shifted(m, step % SIDE, 0) if axis == "z" else shifted(m, 0, step % SIDE)
+
+
+def place(m, h, first, second):
+    if h == 0:
+        return shifted(m, second % SIDE, first % SIDE)
+    return shifted(m, first % SIDE, second % SIDE)
+
+
+AXES = (("y", "z"), ("z", "y"))
+ARRIVALS = [(-1, 0), (1, 0), (0, -1), (0, 1), (2, 0), (-1, -1), (-1, 1), (1, -1), (1, 1),
+            (0, 2), (2, -1), (2, 1), (-1, 2), (1, 2), (2, 2)]
+
+
+class Spread:
+    def __init__(self, m, slot, recv, send, landed=None):
+        self.m, self.slot, self.recv, self.send = m, slot, recv, send
+        self.landed = landed
+        self.sends = []
+        self.step = 0
+
+    def put(self, h, a, b, q, which, by, device=None, source=None):
+        origin = place(self.m, h, a, b)
+        there = (a - by, b) if which == 0 else (a, b - by)
+        key = (there[0] % SIDE) * SIDE + there[1] % SIDE
+        ref = self.slot(origin, h, q)
+        target = {"mp": near(self.m, AXES[h][which], by)}
+        if device:
+            target.update(device)
+        copy = remote(ref if source is None else source(h), ref, self.send.at[len(self.sends)],
+                      self.recv.at[h, key, q or 0], target)
+        copy.start()
+        self.sends.append(copy)
+
+    def own(self, device=None, source=None):
+        for which in (0, 1):
+            for h in (0, 1):
+                for by in (1, -1):
+                    self.put(h, 0, 0, None, which, by, device, source)
+
+    def take(self, h, a, b, q):
+        ref = self.slot(place(self.m, h, a, b), h, q)
+        key = (a % SIDE) * SIDE + b % SIDE
+        remote(ref, ref, self.send.at[0], self.recv.at[h, key, q or 0],
+               {"mp": near(self.m, "y", 1)}).wait_recv()
+
+    def pass_on(self, until=len(ARRIVALS)):
+        for a, b in ARRIVALS[self.step:until]:
+            for h in (0, 1):
+                if b == 2 or (b == 0 and a == 2):
+                    self.take(h, a, b, 0)
+                    self.take(h, a, b, 1)
+                else:
+                    self.take(h, a, b, None)
+                if b == 0:
+                    if a == -1:
+                        self.put(h, a, b, 0, 0, 1)
+                    if a == 1:
+                        self.put(h, a, b, 1, 0, -1)
+                    self.put(h, a, b, None, 1, 1)
+                    self.put(h, a, b, None, 1, -1)
+                if b == -1:
+                    self.put(h, a, b, 0, 1, 1)
+                if b == 1:
+                    self.put(h, a, b, 1, 1, -1)
+                if self.landed:
+                    self.landed(h, a, b)
+        self.step = until
+
+    def close(self):
+        for copy in self.sends:
+            copy.wait_send()
+
+
+ORDER = (2, 1, 3, 0)
+DIRS = (1, -1)
+
+
+def gather_sum_scratch(quarter):
+    dma = pltpu.SemaphoreType.DMA
+    return [
+        VMEM((2, 2, SIDE) + quarter, BF), VMEM((2, 2, 2, SIDE) + quarter, BF),
+        VMEM((2, 2, SIDE) + quarter, BF),
+        VMEM((2, 2) + quarter, BF), VMEM((2, 2, 2) + quarter, BF), VMEM((2, 2) + quarter, BF),
+        VMEM((2, 2, SIDE) + quarter, BF),
+        dma((2, 2, SIDE)), dma((2, 2, 2, SIDE)), dma((2, 2)), dma((2, 2, 2)), dma((64,)),
+    ]
+
+
+def gather_sum(m, slot, load, scratch, begin=None):
+    far1, near1, add1, far2, near2, add2, mid, far1_r, near1_r, far2_r, near2_r, send = scratch
+    sends = []
+
+    def put(src, dst, recv, h, which, by):
+        copy = remote(src, dst, send.at[len(sends)], recv, {"mp": near(m, AXES[h][which], by)})
+        copy.start()
+        sends.append(copy)
+
+    def take(dst, recv):
+        remote(dst, dst, send.at[0], recv, {"mp": near(m, "y", 1)}).wait_recv()
+
+    def owner(h, a, b):
+        return place(m, h, a, b)
+
+    for b in ORDER:
+        if begin:
+            begin(b)
+        for h in (0, 1):
+            for i, by in enumerate(DIRS):
+                put(slot(owner(h, 2, b), h, i), far1.at[h, i, b], far1_r.at[h, i, b], h, 0, by)
+        for h in (0, 1):
+            for i, by in enumerate(DIRS):
+                put(slot(owner(h, by, b), h, 1 - i), near1.at[h, i, 1 - i, b],
+                    near1_r.at[h, i, 1 - i, b], h, 0, by)
+    for b in ORDER:
+        for h in (0, 1):
+            for i, by in enumerate(DIRS):
+                take(far1.at[h, i, b], far1_r.at[h, i, b])
+                add1[h, i, b] = (far1[h, i, b].astype(F32)
+                                 + load(owner(h, by, b), h, i).astype(F32)).astype(BF)
+                put(add1.at[h, i, b], near1.at[h, i, i, b], near1_r.at[h, i, i, b], h, 0, by)
+
+    def first(h, q, b):
+        total = load(owner(h, 0, b), h, q).astype(F32)
+        for i in (0, 1):
+            take(near1.at[h, i, q, b], near1_r.at[h, i, q, b])
+            total = total + near1[h, i, q, b].astype(F32)
+        return total
+
+    for b in ORDER[:3]:
+        for h in (0, 1):
+            for q in (1, 0):
+                mid[h, q, b] = first(h, q, b).astype(BF)
+                if b == 2:
+                    put(mid.at[h, q, b], far2.at[h, q], far2_r.at[h, q], h, 1, DIRS[q])
+                else:
+                    i = 0 if b == 1 else 1
+                    if q != i:
+                        put(mid.at[h, q, b], near2.at[h, i, q], near2_r.at[h, i, q], h, 1, DIRS[i])
+    for h in (0, 1):
+        for i, by in enumerate(DIRS):
+            take(far2.at[h, i], far2_r.at[h, i])
+            add2[h, i] = (far2[h, i].astype(F32) + mid[h, i, by % SIDE].astype(F32)).astype(BF)
+            put(add2.at[h, i], near2.at[h, i, i], near2_r.at[h, i, i], h, 1, by)
+    sums = {}
+    for h in (0, 1):
+        for q in (0, 1):
+            sums[h, q] = first(h, q, 0)
+    for h in (0, 1):
+        for q in (0, 1):
+            for i in (0, 1):
+                take(near2.at[h, i, q], near2_r.at[h, i, q])
+                sums[h, q] = sums[h, q] + near2[h, i, q].astype(F32)
+    return sums, sends
+
+
+def neighbours_of(m):
+    return [near(m, axis, by) for axis in ("y", "z") for by in (1, -1)]
+
+
 def encode_kernel(
     x_ref, wo_ref, ed_ref, pool_ref, gain_ref, up_ref,
     enc_ref, xf_ref, wor_ref,
-    edr, dt, hid, part, rs,
-    own_sem, ed_s, ed_r, x_s, x_r, wo_s, wo_r, rs_s, rs_r, ag_s, ag_r, fw_s, fw_r,
+    edr, dt, hid, part,
+    own_sem, ed_s, ed_r, wo_s, wo_r, x_s, x_r, ag_s, ag_r, fw_s, fw_r, *scratch,
 ):
     s = lax.axis_index("section")
     m = lax.axis_index("mp")
@@ -98,9 +259,16 @@
         sends.append(remote(wo_ref.at[rows_of(p, span), :], wor_ref.at[:, cols],
                             wo_s.at[k], wo_r.at[k], {"mp": p}))
         sends[-1].start()
-        sends.append(remote(x_ref, xf_ref.at[:, cols], x_s.at[k], x_r.at[k], {"mp": p}))
-        sends[-1].start()
-
+
+    tall = x_ref.shape[0]
+
+    def x_rows(h, q):
+        if q is None:
+            return pl.ds(h * (tall // 2), tall // 2)
+        return pl.ds((2 * h + q) * (tall // 4), tall // 4)
+
+    xs = Spread(m, lambda owner, h, q: xf_ref.at[x_rows(h, q), rows_of(owner, HEAD)], x_r, x_s)
+    xs.own(None, lambda h: x_ref.at[x_rows(h, None), :])
     gain = gain_ref[...]
 
     def hidden_rows(i, carry):
@@ -120,56 +288,66 @@
     for p in range(len(edr)):
         dt[pl.ds(p * feat, feat), :] = edr[p, pl.ds(0, feat), :].astype(F32)
     down = dt[...].astype(BF)
-    shard = rs.shape[1]
-    for dz in (2, 1, 3, 0):
-        block = rows_of(lax.rem(lax.div(m, SIDE) + dz, SIDE), SIDE * shard)
+    shard = part.shape[0] // len(edr)
+
+    def rows_at(owner, h, q, base=0):
+        if q is None:
+            return pl.ds(pl.multiple_of((base + owner) * shard + h * (shard // 2), shard // 2),
+                         shard // 2)
+        return pl.ds(pl.multiple_of((base + owner) * shard + (2 * h + q) * (shard // 4), shard // 4),
+                     shard // 4)
+
+    def some(i, carry):
+        block = rows_of(i, SIDE * shard)
         part[block, :] = mul(hid[block, :], down, 1, 1).astype(BF)
-        for k in range(count):
-            if OFFSETS[k][0] != dz:
-                continue
-            p = to_peer(m, k)
-            sends.append(remote(part.at[rows_of(p, shard), :], rs.at[k],
-                                rs_s.at[k], rs_r.at[k], {"mp": p}))
-            sends[-1].start()
-    mine = rows_of(m, shard)
-    total = pool_ref[mine, :].astype(F32) + part[mine, :].astype(F32)
-    for k in range(count):
-        p = from_peer(m, k)
-        remote(part.at[rows_of(p, shard), :], rs.at[k], rs_s.at[k], rs_r.at[k], {"mp": p}).wait_recv()
-        total = total + rs[k].astype(F32)
+        return carry
+
+    lax.fori_loop(0, SIDE, some, 0)
+    xs.pass_on(5)
+    sums, more = gather_sum(m, lambda owner, h, q: part.at[rows_at(owner, h, q), :],
+                            lambda owner, h, q: part[rows_at(owner, h, q), :], scratch)
     half = s * len(edr)
-    place = rows_of(half + m, shard)
-    enc_ref[place, :] = total.astype(BF)
-    for k in range(count):
-        p = to_peer(m, k)
-        sends.append(remote(enc_ref.at[place, :], enc_ref.at[place, :],
-                            ag_s.at[k], ag_r.at[k], {"mp": p}))
-        sends[-1].start()
-    sends.append(remote(enc_ref.at[place, :], enc_ref.at[place, :],
-                        fw_s.at[count], fw_r.at[count], other))
-    sends[-1].start()
-    for k in reversed(range(count)):
-        p = from_peer(m, k)
-        there = rows_of(half + p, shard)
-        remote(enc_ref.at[there, :], enc_ref.at[there, :], ag_s.at[k], ag_r.at[k], {"mp": p}).wait_recv()
-        sends.append(remote(enc_ref.at[there, :], enc_ref.at[there, :],
-                            fw_s.at[k], fw_r.at[k], other))
-        sends[-1].start()
+
+    def enc_slot(owner, h, q):
+        return enc_ref.at[rows_at(owner, h, q, half), :]
+
+    for h in (0, 1):
+        for q in (0, 1):
+            total = pool_ref[rows_at(m, h, q), :].astype(F32) + sums[h, q]
+            enc_ref[rows_at(m, h, q, half), :] = total.astype(BF)
+
+    def to_other(h, a, b):
+        key = (a % SIDE) * SIDE + b % SIDE
+        ref = enc_slot(place(m, h, a, b), h, None)
+        more.append(remote(ref, ref, fw_s.at[h, key], fw_r.at[h, key], other))
+        more[-1].start()
+
+    spread = Spread(m, enc_slot, ag_r, ag_s, to_other)
+    spread.own()
+    to_other(0, 0, 0)
+    to_other(1, 0, 0)
+    spread.pass_on(5)
+    xs.pass_on(9)
+    spread.pass_on(9)
+    xs.pass_on()
+    spread.pass_on()
     away = (1 - s) * len(edr)
-    for k in range(count + 1):
-        p = m if k == count else from_peer(m, k)
-        there = rows_of(away + p, shard)
-        remote(enc_ref.at[there, :], enc_ref.at[there, :], fw_s.at[k], fw_r.at[k], other).wait_recv()
+    for a, b in [(0, 0)] + ARRIVALS:
+        for h in (0, 1):
+            key = (a % SIDE) * SIDE + b % SIDE
+            ref = enc_ref.at[rows_at(place(m, h, a, b), h, None, away), :]
+            remote(ref, ref, fw_s.at[h, key], fw_r.at[h, key], other).wait_recv()
     for k in range(count):
         p = from_peer(m, k)
         there = rows_of(p, HEAD)
         remote(wo_ref.at[rows_of(p, span), :], wor_ref.at[:, there],
                wo_s.at[k], wo_r.at[k], {"mp": p}).wait_recv()
-        remote(x_ref, xf_ref.at[:, there], x_s.at[k], x_r.at[k], {"mp": p}).wait_recv()
     own[0].wait()
     own[1].wait()
-    for copy in sends:
+    for copy in sends + more:
         copy.wait_send()
+    spread.close()
+    xs.close()
 
 
 def encode(x, wo, ed, pool, gain, up):
@@ -191,9 +369,10 @@
         out_specs=(vmem,) * 3,
         scratch_shapes=[
             VMEM(ed.shape, BF), VMEM((enc, span), F32), VMEM((rows, span), BF),
-            VMEM((rows, enc), BF), VMEM((count, rows // peers, enc), BF),
+            VMEM((rows, enc), BF),
             dma((3,)),
-        ] + [dma((count,))] * 10 + [dma((count + 1,))] * 2,
+        ] + [dma((count,))] * 4 + [dma((40,)), dma((2, 16, 2))] * 2 + [dma((2, 16))] * 2
+        + gather_sum_scratch((rows // peers // 4, enc)),
         compiler_params=pltpu.CompilerParams(
             collective_id=0, has_side_effects=True, vmem_limit_bytes=LIMIT),
     )(x, wo, ed, pool, gain, up)
@@ -361,65 +540,61 @@
 
 
 def relay_kernel(from_section, combine, *refs):
-    part_ref, row_refs, full_ref = refs[0], refs[1:-8], refs[-8]
-    rs, done, rs_s, rs_r, ag_s, ag_r = refs[-7:-1]
+    outer = len(refs) - 1 - 12 - 5
+    part_ref, row_refs, full_ref = refs[0], refs[1:outer], refs[outer]
+    done, hand_s, hand_r, ag_s, ag_r = refs[outer + 1:outer + 6]
+    scratch = refs[outer + 6:]
     s = lax.axis_index("section")
     m = lax.axis_index("mp")
-    count = len(OFFSETS)
     there = {"section": 1 - s}
-    everyone = [{"mp": to_peer(m, k)} for k in range(count)]
-    everyone += [{"mp": to_peer(m, k), "section": 1 - s} for k in range(count)]
-    greet(everyone + [there])
-    shard = rs.shape[1]
+    greet([{"mp": p} for p in neighbours_of(m)]
+          + [{"mp": p, "section": 1 - s} for p in neighbours_of(m)] + [there])
+    shard, width = done.shape
     mine = rows_of(m, shard)
+
+    def columns(h, q):
+        if q is None:
+            return pl.ds(h * (width // 2), width // 2)
+        return pl.ds((2 * h + q) * (width // 4), width // 4)
+
+    def slot(ref):
+        return lambda owner, h, q: ref.at[rows_of(owner, shard), columns(h, q)]
 
     @pl.when(s == from_section)
     def _():
-        sends = []
-        for k in range(count):
-            p = to_peer(m, k)
-            sends.append(remote(part_ref.at[rows_of(p, shard), :], rs.at[k],
-                                rs_s.at[k], rs_r.at[k], {"mp": p}))
-            sends[-1].start()
-        total = part_ref[mine, :].astype(F32)
-        for k in range(count):
-            p = from_peer(m, k)
-            remote(part_ref.at[rows_of(p, shard), :], rs.at[k],
-                   rs_s.at[k], rs_r.at[k], {"mp": p}).wait_recv()
-            total = total + rs[k].astype(F32)
+        sums, sends = gather_sum(m, slot(part_ref),
+                                 lambda owner, h, q: part_ref[rows_of(owner, shard), columns(h, q)],
+                                 scratch)
+        total = jnp.concatenate([sums[h, q] for h in (0, 1) for q in (0, 1)], axis=1)
         done[...] = combine(total, mine, *row_refs).astype(BF)
-        for k in range(count + 1):
-            device = there if k == count else {"mp": to_peer(m, k), "section": 1 - s}
-            sends.append(remote(done, full_ref.at[mine, :], ag_s.at[k], ag_r.at[k], device))
-            sends[-1].start()
-        for copy in sends:
+        spread = Spread(m, slot(full_ref), ag_r, ag_s)
+        spread.own(there, lambda h: done.at[:, columns(h, None)])
+        hand = remote(done, full_ref.at[mine, :], hand_s.at[0], hand_r.at[0], there)
+        hand.start()
+        for copy in sends + [hand]:
             copy.wait_send()
+        spread.close()
 
     @pl.when(s != from_section)
     def _():
-        for k in range(count + 1):
-            p = m if k == count else from_peer(m, k)
-            device = there if k == count else {"mp": p, "section": 1 - s}
-            remote(done, full_ref.at[rows_of(p, shard), :],
-                   ag_s.at[k], ag_r.at[k], device).wait_recv()
+        spread = Spread(m, slot(full_ref), ag_r, ag_s)
+        spread.pass_on()
+        remote(done, full_ref.at[mine, :], hand_s.at[0], hand_r.at[0], there).wait_recv()
+        spread.close()
 
 
 def relay(from_section, combine, part, rows, ident, peers):
     dma = pltpu.SemaphoreType.DMA
-    count = len(OFFSETS)
     vmem = pl.BlockSpec(memory_space=VMEM)
-    shard = part.shape[0] // peers
+    shard, width = part.shape[0] // peers, part.shape[1]
     return pl.pallas_call(
         functools.partial(relay_kernel, from_section, combine),
         name="relay_%d" % ident,
         out_shape=jax.ShapeDtypeStruct(part.shape, BF),
         in_specs=[vmem] * (1 + len(rows)),
         out_specs=vmem,
-        scratch_shapes=[
-            VMEM((count, shard, part.shape[1]), BF), VMEM((shard, part.shape[1]), BF),
-            dma((count,)), dma((count,)), dma((count + 1,)), dma((count + 1,)),
-            VMEM((8, 128), F32),
-        ],
+        scratch_shapes=[VMEM((shard, width), BF), dma((1,)), dma((1,)), dma((40,)),
+                        dma((2, 16, 2))] + gather_sum_scratch((shard, width // 4)),
         compiler_params=pltpu.CompilerParams(
             collective_id=ident, has_side_effects=True, vmem_limit_bytes=LIMIT),
     )(part, *rows)

time: 276 us -> 234 us (0.85)
  Pallas kernels: 264 us -> 222 us
    pallas_call x1, Pallas kernels: 107 us -> 76 us  [encode(): pl.pallas_call(encode_kernel, name='encode_exchange', out_shape=(jax.Shap...]
    pallas_call x2, Pallas kernels: 96.9 us -> 85.4 us  [relay(): pl.pallas_call(functools.partial(relay_kernel, from_section, combine), na...]
where the time goes in v2:
time: 234 us
  Pallas kernels  222 us (95%)
  local copies, waits for them, and re-layouts  7.99 us (3%)
  other arithmetic  2.92 us (1%)
    pallas_call x2, Pallas kernels, relay(): pl.pallas_call(functools.partial(relay_kernel, from_section, combine), na...  85.4 us
    pallas_call x1, Pallas kernels, encode(): pl.pallas_call(encode_kernel, name='encode_exchange', out_shape=(jax.Shap...  76 us
    pallas_call x3, Pallas kernels, local(): pl.pallas_call(kernel, name=name, out_shape=tuple((jax.ShapeDtypeStruct(*...  41.2 us
    pallas_call x1, Pallas kernels, settle(): pl.pallas_call(settle_kernel, name='settle', out_shape=(jax.ShapeDtypeStr...  19.7 us

profile of v2, /device:TPU:0, one launch (start us, length us, event | category | flops | bytes accessed | tf_op | source)
XLA Modules:
  0.0 233.9 jit_solution(12330748661733278869)
XLA Ops:
  0.6 0.5 broadcast.8
  1.1 1.3 reduce.3
  2.5 0.7 reshape_squeeze.10.used_ref
  3.2 1.3 broadcast_in_dim.9.gain_ref
  4.4 1.6 broadcast_select_fusion
  6.0 1.0 copy.27
  7.1 0.9 pad.4.ed_ref
  7.9 76.0 %encode_exchange.1 = (bf16[2048,896]{1,0:T(8,128)(2,1)}, bf16[512,2048]{1,0:T(8,128)(2,1)}, bf16[256,2048]{1,0:T(8,128)(2,1)}) custom-call(bf16[512,128]{1,0:T(8,128)(2,1)} %bitcast.21, bf16[4096,128]{1,0:T(8,128)(2,1)} %bitcast.20, bf16[16,64,256]{2,1,0:T(8,128)(2,1)} %pad.4.ed_ref, bf16[1024,896]{1,0:T(8,128)(2,1)} %bitcast.19, ...), custom_call_target="tpu_custom_call" | custom-call | tf_op jit(solution)/shard_map/encode_exchange/pallas_call | solution.py:360
  84.0 19.0 %front.1 = (bf16[2048,256]{1,0:T(8,128)(2,1)}, bf16[2048,256]{1,0:T(8,128)(2,1)}, bf16[512,256]{1,0:T(8,128)(2,1)}, f32[8,2,64,512]{3,2,1,0:T(8,128)}, bf16[512,...) custom-call(s32[8,4]{1,0:T(8,128)} %bitcast.27, s32[8]{0:T(128)} %reshape_squeeze.10.used_ref, ...), custom_call_target="tpu_custom_call" | custom-call | tf_op jit(solution)/shard_map/front/pallas_call | solution.py:672
  103.0 24.1 %relay_1.1.x_ref.refs_1_ = bf16[512,2048]{1,0:T(8,128)(2,1)} custom-call(bf16[512,2048]{1,0:T(8,128)(2,1)} %get-tuple-element.21.refs_0_, bf16[512,2048]{1,0:T(8,128)(2,1)} %get-tuple-element.18.x_ref.refs_1_.refs_2_), custom_call_target="tpu_custom_call" | custom-call | tf_op jit(solution)/shard_map/relay_1/pallas_call | solution.py:590
  127.1 5.2 %late.1 = (bf16[512,2048]{1,0:T(8,128)(2,1)}, bf16[896,256]{1,0:T(8,128)(2,1)}, bf16[896,256]{1,0:T(8,128)(2,1)}) custom-call(s32[8,4]{1,0:T(8,128)} %bitcast.28, s32[8]{0:T(128)} %reshape_squeeze.10.used_ref, bf16[512,2048]{1,0:T(8,128)(2,1)} %relay_1.1.x_ref.refs_1_, f32[1,2048]{1,0:T(1,128)} %refs_3_.1, bf16[2048,256]{1,0:T(8,128)(2,1)} %bitcast.17, ...), custom_call_target="tpu_custom_call" | custom-call | tf_op jit(solution)/shard_map/late/pallas_call | solution.py:672
  132.3 61.4 %relay_2.1.g_ref = bf16[512,2048]{1,0:T(8,128)(2,1)} custom-call(bf16[512,2048]{1,0:T(8,128)(2,1)} %get-tuple-element.25.refs_0_, bf16[512,2048]{1,0:T(8,128)(2,1)} %relay_1.1.x_ref.refs_1_, bf16[512,2048]{1,0:T(8,128)(2,1)} %get-tuple-element.18.x_ref.refs_1_.refs_2_, f32[1,2048]{1,0:T(1,128)} %refs_3_.1), custom_call_target="tpu_custom_call" | custom-call | tf_op jit(solution)/shard_map/relay_2/pallas_call | solution.py:590
  193.7 16.9 %early.1 = (bf16[896,256]{1,0:T(8,128)(2,1)}, bf16[896,256]{1,0:T(8,128)(2,1)}) custom-call(s32[8,4]{1,0:T(8,128)} %bitcast.29, bf16[512,2048]{1,0:T(8,128)(2,1)} %relay_2.1.g_ref, bf16[256,2048]{1,0:T(8,128)(2,1)} %get-tuple-element.20.wor_ref, bf16[2048,896]{1,0:T(8,128)(2,1)} %get-tuple-element.19.enc_ref, bf16[2048,256]{1,0:T(8,128)(2,1)} %get-tuple-element.23.v_ref, ...), custom_call_target="tpu_custom_call" | custom-call | tf_op jit(solution)/shard_map/early/pallas_call | solution.py:672
  210.6 19.7 %settle.1 = (bf16[896,256]{1,0:T(8,128)(2,1)}, bf16[896,256]{1,0:T(8,128)(2,1)}) custom-call(bf16[896,256]{1,0:T(8,128)(2,1)} %get-tuple-element.30.k_ref, bf16[896,256]{1,0:T(8,128)(2,1)} %get-tuple-element.31.v_ref), custom_call_target="tpu_custom_call" | custom-call | tf_op jit(solution)/shard_map/settle/pallas_call | solution.py:656
  230.3 1.8 copy.30
  232.1 1.8 copy.31
